TPU v7x, 256 devices: a whole 4x4x8 slice. The times are simulated.
256 devices in a mesh: row: 8 (over x, core), col: 32 (over z, y).
Axes of the slice: x: 4, y: 4, z: 8, core: 2. Of those that a mesh axis runs over, the one named last changes fastest.
Arguments:
- layer_input: bfloat16 [16896, 1024], P('col', 'row'), may hold values from -6 to 6
- w_q: bfloat16 [1024, 1024], P('col', 'row'), may hold values from -0.1875 to 0.1875
- w_k: bfloat16 [1024, 1024], P('col', 'row'), may hold values from -0.1875 to 0.1875
- w_v: bfloat16 [1024, 1024], P('col', 'row'), may hold values from -0.1875 to 0.1875
- w_o: bfloat16 [1024, 1024], P('row', 'col'), may hold values from -0.375 to 0.375
- w_gate: bfloat16 [1024, 4096], P('col', 'row'), may hold values from -0.1875 to 0.1875
- w_up: bfloat16 [1024, 4096], P('col', 'row'), may hold values from -0.1875 to 0.1875
- w_down: bfloat16 [4096, 1024], P('row', 'col'), may hold values from -0.1875 to 0.1875
- norm1: float32 [1024], replicated, may hold values from 0.5 to 1.5
- norm2: float32 [1024], replicated, may hold values from 0.5 to 1.5
- q_gain: float32 [1024], P('row'), may hold values from 0.5 to 1.5
- k_gain: float32 [1024], P('row'), may hold values from 0.5 to 1.5
- bias_same: float32 [16], P('row'), may hold values from -3 to 3
- bias_diff: float32 [16], P('row'), may hold values from -3 to 3
- pre_variate: int32 [32, 512], P('col'), may hold values from 0 to 7, never falling along the last dimension, each value on 1 to 128 neighbouring positions
- pre_keep: int32 [32, 512], P('col'), may hold values 0 or 1
- dec_variate: int32 [512], P('col'), may hold values from 0 to 7
- dec_len: int32 [512], P('col'), may hold values from 1 to 1023, as said below
- dec_table: int32 [512, 8], P('col'), may hold values from 0 to 31
- dec_holder: int32 [512, 1], P('col'), may hold values from 0 to 31; in each aligned block of 16 rows (0 to 15, 16 to 31, ...) at most 2 rows name the same one
- kv_pool: bfloat16 [1024, 2, 128, 1024], P('col', None, None, 'row'), may hold values from -4 to 4
- page_variates: int32 [1024, 128], P('col'), may hold values from 0 to 7
Outputs:
- hidden: bfloat16 [16896, 1024], P('col', 'row')
- prefill_pages: bfloat16 [128, 2, 128, 1024], P('col', None, None, 'row')
- tail_pages: bfloat16 [512, 2, 128, 1024], P('col', None, None, 'row')
Inputs may be any that keep to these rules, and one draw needn't show every extreme that they name: `pre_variate`: each variate's tokens form one run of at most 128 positions. `dec_len`: some request has exactly 1023 cached tokens. `dec_table`: entries past a request's last page are unused; requests may share pages. `dec_holder`: among the 16 requests of one column group at most 2 name the same holder, a bound that some block reaches of them.
All inputs are finite; a program needn't handle non-finite values. No bound on the sum of `pre_keep` on one device may be relied on, other than what follows from the above.
Results may differ from a plain program's by a relative error of at most 0.015.
Values may be sent and summed in bfloat16 or wider, within the bound.
No kernel may reach another device: no remote copies, remote signals or barrier semaphores. Data moves between devices by JAX's collectives and lax.ppermute only.
A program may use at most 128 MiB of HBM per device.

v0:
```python
import jax
import jax.numpy as jnp
from jax import lax
from jax.sharding import PartitionSpec as P

HD = 64
eps = 1e-05


def as_sent(array):
    return jax.tree.map(lambda a: a.astype(jnp.bfloat16) if a.dtype == jnp.float32 else a, array)


def norm_rows(values, gain_row):
    return values * lax.rsqrt(jnp.mean(values * values, axis=-1, keepdims=True) + eps) * gain_row


def rotate(tensor, places):
    half_size = tensor.shape[-1] // 2
    spacing = jnp.arange(half_size).astype(jnp.float32) * (2.0 / tensor.shape[-1])
    angles = places.astype(jnp.float32)[:, None] * jnp.power(10000.0, -spacing)[None, :]
    cosine = jnp.cos(angles)[:, None, :]
    sine_part = jnp.sin(angles)[:, None, :]
    lower_half = tensor[..., :half_size]
    upper_half = tensor[..., half_size:]
    return jnp.concatenate(
        [
            lower_half * cosine - upper_half * sine_part,
            upper_half * cosine + lower_half * sine_part,
        ],
        axis=-1,
    )


def segment_time(variates):
    places = jnp.arange(variates.shape[0])
    run_start = jnp.concatenate([jnp.ones((1,), dtype=jnp.bool_), variates[1:] != variates[:-1]])
    starts = lax.cummax(jnp.where(run_start, places, 0), axis=0)
    return places - starts


def on_device(
    layer_input,
    w_q,
    w_k,
    w_v,
    w_o,
    w_gate,
    w_up,
    w_down,
    norm1,
    norm2,
    q_gain,
    k_gain,
    bias_same,
    bias_diff,
    pre_variate,
    pre_keep,
    dec_variate,
    dec_len,
    dec_table,
    dec_holder,
    kv_pool,
    page_variates,
):
    row_count = layer_input.shape[0]
    local_width = layer_input.shape[1]
    pre_len = pre_variate.shape[1]
    dec_count = dec_len.shape[0]
    heads_here = local_width // HD
    score_scale = HD ** (-0.5)
    page_size = kv_pool.shape[2]
    page_count = dec_table.shape[1]
    gathered_input = lax.all_gather(layer_input, "row", axis=1, tiled=True)
    normed = norm_rows(gathered_input.astype(jnp.float32), norm1).astype(jnp.bfloat16)
    pieces = (
        lax.all_gather(w_q, "col", axis=0, tiled=True),
        lax.all_gather(w_k, "col", axis=0, tiled=True),
        lax.all_gather(w_v, "col", axis=0, tiled=True),
    )
    columns = normed
    queries = jnp.dot(columns, pieces[0], preferred_element_type=jnp.float32)
    keys_proj = jnp.dot(columns, pieces[1], preferred_element_type=jnp.float32)
    values_proj = jnp.dot(columns, pieces[2], preferred_element_type=jnp.float32)
    places = jnp.concatenate([segment_time(pre_variate[0]), dec_len])
    query_rot = rotate(
        norm_rows(queries.reshape(row_count, heads_here, HD), q_gain.reshape(heads_here, HD)),
        places,
    ).astype(jnp.bfloat16)
    key_rot = rotate(
        norm_rows(keys_proj.reshape(row_count, heads_here, HD), k_gain.reshape(heads_here, HD)),
        places,
    ).astype(jnp.bfloat16)
    value_bf = values_proj.astype(jnp.bfloat16).reshape(row_count, heads_here, HD)

    def attend_slot(inputs):
        float_item, int_item = inputs
        new_query = float_item[:local_width].reshape(heads_here, HD)
        new_key = float_item[local_width : 2 * local_width]
        new_value = float_item[2 * local_width :]
        page_rows = int_item[:page_count]
        length = int_item[page_count]
        variate = int_item[page_count + 1]
        gathered = kv_pool[page_rows]
        cached_keys = gathered[:, 0].reshape(page_count * page_size, heads_here, HD)
        cached_vals = gathered[:, 1].reshape(page_count * page_size, heads_here, HD)
        key_variates = page_variates[page_rows].reshape(page_count * page_size)
        scores = (
            jnp.einsum("hd,khd->hk", new_query, cached_keys, preferred_element_type=jnp.float32)
            * score_scale
        )
        scores = scores + jnp.where(
            (key_variates == variate)[None, :], bias_same[:, None], bias_diff[:, None]
        )
        key_heads = new_key.reshape(heads_here, HD)
        value_heads = new_value.reshape(heads_here, HD)
        own_score = (
            jnp.sum(new_query.astype(jnp.float32) * key_heads.astype(jnp.float32), axis=1)
            * score_scale
            + bias_same
        )
        exp_scores = jnp.where(
            (jnp.arange(page_count * page_size) < length)[None, :], jnp.exp(scores), 0.0
        )
        own_exp = jnp.exp(own_score)
        total_weight = jnp.sum(exp_scores, axis=1) + own_exp
        weights_bf = (exp_scores / total_weight[:, None]).astype(jnp.bfloat16)
        own_weight = (own_exp / total_weight).astype(jnp.bfloat16)
        attended = jnp.einsum(
            "hk,khd->hd", weights_bf, cached_vals, preferred_element_type=jnp.float32
        ) + own_weight.astype(jnp.float32)[:, None] * value_heads.astype(jnp.float32)
        tail_slot = page_rows[length // page_size]
        old_page = kv_pool[tail_slot]
        hit_row = (jnp.arange(page_size) == length % page_size)[None, :, None]
        new_rows = jnp.stack([new_key, new_value])[:, None, :]
        return (
            attended.astype(jnp.bfloat16).reshape(local_width),
            jnp.where(hit_row, new_rows, old_page),
        )

    keep_mask = pre_keep[0]
    variates = pre_variate[0]
    block_rows = min(512, pre_len)
    pre_keys = key_rot[:pre_len]
    pre_values = value_bf[:pre_len]
    block_queries = query_rot[0:block_rows]
    scores = (
        jnp.einsum("qhd,khd->hqk", block_queries, pre_keys, preferred_element_type=jnp.float32)
        * score_scale
    )
    same_var = variates[0:block_rows, None] == variates[None, :]
    scores = scores + jnp.where(same_var[None], bias_same[:, None, None], bias_diff[:, None, None])
    allowed = (keep_mask[None, :] == 1) | (
        jnp.arange(0, block_rows)[:, None] == jnp.arange(pre_len)[None, :]
    )
    exp_scores = jnp.where(allowed[None], jnp.exp(scores), 0.0)
    weights_bf = (exp_scores / jnp.sum(exp_scores, axis=2, keepdims=True)).astype(jnp.bfloat16)
    outputs = jnp.einsum(
        "hqk,khd->qhd", weights_bf, pre_values, preferred_element_type=jnp.float32
    ).astype(jnp.bfloat16)
    prefill_out = outputs.reshape(pre_len, local_width)
    peer_count = lax.axis_size("col")
    slot_count = max(2, (dec_count + peer_count - 1) // peer_count)
    holder = dec_holder[:, 0]
    onehot = (holder[:, None] == jnp.arange(peer_count)[None, :]).astype(jnp.int32)
    slot_rank = jnp.sum((jnp.cumsum(onehot, axis=0) - onehot) * onehot, axis=1)
    target = holder * slot_count + slot_rank
    payload = jnp.concatenate(
        [
            query_rot[pre_len:].reshape(dec_count, local_width),
            key_rot[pre_len:].reshape(dec_count, local_width),
            value_bf[pre_len:].reshape(dec_count, local_width),
        ],
        axis=1,
    )
    int_facts = jnp.concatenate([dec_table, dec_len[:, None], dec_variate[:, None]], axis=1)
    send_float = (
        jnp.zeros((peer_count * slot_count, 3 * local_width), jnp.bfloat16).at[target].set(payload)
    )
    send_int = (
        jnp.zeros((peer_count * slot_count, page_count + 2), jnp.int32).at[target].set(int_facts)
    )
    send_float = send_float.reshape(peer_count, slot_count, 3 * local_width)
    send_int = send_int.reshape(peer_count, slot_count, page_count + 2)
    floats = lax.all_to_all(send_float, "col", split_axis=0, concat_axis=0, tiled=True)
    int_part = lax.all_to_all(send_int, "col", split_axis=0, concat_axis=0, tiled=True)
    group_count = floats.shape[0]
    item_count = floats.shape[1]
    flat_floats = floats.reshape(group_count * item_count, floats.shape[2])
    flat_ints = int_part.reshape(group_count * item_count, int_part.shape[2])
    batch_slots = min(16, group_count * item_count)
    slot_out, slot_tail = lax.map(attend_slot, (flat_floats, flat_ints), batch_size=batch_slots)
    slot_out = slot_out.reshape(group_count, item_count, local_width)
    slot_tail = slot_tail.reshape(group_count, item_count, 2, page_size, local_width)
    back_out = lax.all_to_all(
        as_sent(slot_out), "col", split_axis=0, concat_axis=0, tiled=True
    ).astype(slot_out.dtype)
    back_tail = lax.all_to_all(
        as_sent(slot_tail), "col", split_axis=0, concat_axis=0, tiled=True
    ).astype(slot_tail.dtype)
    decode_out = back_out.reshape(peer_count * slot_count, local_width)[target]
    tails = back_tail.reshape(peer_count * slot_count, 2, page_size, local_width)[target]
    decode_out, tail_pages = (decode_out, tails)
    all_attended = jnp.concatenate([prefill_out, decode_out], axis=0)
    partial_out = jnp.dot(
        all_attended,
        lax.all_gather(w_o, "col", axis=1, tiled=True),
        preferred_element_type=jnp.float32,
    )
    share_start = lax.axis_index("row") * local_width
    attn_total = lax.psum(partial_out.astype(jnp.bfloat16), "row").astype(jnp.float32)
    resid_full = gathered_input.astype(jnp.float32) + attn_total
    ffn_input = norm_rows(resid_full, norm2).astype(jnp.bfloat16)
    resid_share = lax.dynamic_slice_in_dim(resid_full, share_start, local_width, 1)
    zero_hidden = jnp.zeros((row_count, w_gate.shape[1]), jnp.float32)
    pieces = (
        lax.all_gather(w_gate, "col", axis=0, tiled=True),
        lax.all_gather(w_up, "col", axis=0, tiled=True),
    )
    columns = lax.slice_in_dim(ffn_input, 0, pieces[0].shape[0], axis=1)
    gate_proj = zero_hidden + jnp.dot(columns, pieces[0], preferred_element_type=jnp.float32)
    up_proj = zero_hidden + jnp.dot(columns, pieces[1], preferred_element_type=jnp.float32)
    hidden_units = (jax.nn.silu(gate_proj) * up_proj).astype(jnp.bfloat16)
    partial_ffn = jnp.dot(
        hidden_units,
        lax.all_gather(w_down, "col", axis=1, tiled=True),
        preferred_element_type=jnp.float32,
    )
    ffn_share = lax.psum_scatter(
        partial_ffn.astype(jnp.bfloat16), "row", scatter_dimension=1, tiled=True
    ).astype(jnp.float32)
    hidden = (resid_share + ffn_share).astype(jnp.bfloat16)
    prefill_pages = jnp.stack(
        [
            key_rot[:pre_len].reshape(pre_len // page_size, page_size, local_width),
            value_bf[:pre_len].reshape(pre_len // page_size, page_size, local_width),
        ],
        axis=1,
    )
    return (hidden, prefill_pages, tail_pages)


def solution(mesh):
    placed = (
        P("col", "row"),
        P("col", "row"),
        P("col", "row"),
        P("col", "row"),
        P("row", "col"),
        P("col", "row"),
        P("col", "row"),
        P("row", "col"),
        P(),
        P(),
        P("row"),
        P("row"),
        P("row"),
        P("row"),
        P("col", None),
        P("col", None),
        P("col"),
        P("col"),
        P("col", None),
        P("col", None),
        P("col", None, None, "row"),
        P("col", None),
    )
    return jax.shard_map(
        on_device,
        mesh=mesh,
        in_specs=placed,
        out_specs=(P("col", "row"), P("col", None, None, "row"), P("col", None, None, "row")),
        check_vma=False,
    )
```

profile of v0, /device:TPU:8, one launch (start us, length us, event | category | flops | bytes accessed | tf_op | source)
XLA Modules:
  0.0 774.8 jit_solution(16630199738598560226)
XLA Ops:
  15.8 51.9 %all_gather.27 = bf16[1024,128]{1,0:T(8,128)(2,1)S(1)} all-gather(bf16[32,128]{1,0:T(8,128)(2,1)} %param.26), channel_id=1, replica_groups=mesh['row'=8,'col'=32] {'col'}, dimensions={0}, use_global_device_ids=true | all-gather | bytes 270336 | tf_op jit(solution)/shard_map/all_gather | solution.py:78
  67.7 47.2 %all_gather.26 = bf16[1024,128]{1,0:T(8,128)(2,1)S(1)} all-gather(bf16[32,128]{1,0:T(8,128)(2,1)} %param.25), channel_id=1, replica_groups=mesh['row'=8,'col'=32] {'col'}, dimensions={0}, use_global_device_ids=true | all-gather | bytes 270336 | tf_op jit(solution)/shard_map/all_gather | solution.py:77
  114.9 47.7 %all_gather.25 = bf16[1024,128]{1,0:T(8,128)(2,1)S(1)} all-gather(bf16[32,128]{1,0:T(8,128)(2,1)} %param.27), channel_id=1, replica_groups=mesh['row'=8,'col'=32] {'col'}, dimensions={0}, use_global_device_ids=true | all-gather | bytes 270336 | tf_op jit(solution)/shard_map/all_gather | solution.py:79
  162.6 51.4 %all_gather.28 = bf16[128,1024]{0,1:T(8,128)(2,1)} all-gather(bf16[128,32]{0,1:T(8,128)(2,1)} %param.28), channel_id=1, replica_groups=mesh['row'=8,'col'=32] {'col'}, dimensions={1}, use_global_device_ids=true | all-gather | bytes 270336 | tf_op jit(solution)/shard_map/all_gather | solution.py:207
  223.5 7.1 all-to-all-start.1
  230.6 8.7 %all-to-all-done.1 = bf16[32,2,384]{2,1,0:T(2,128)(2,1)S(1)} async-done(((bf16[32,2,384]{2,1,0:T(2,128)(2,1)}), bf16[32,2,384]{2,1,0:T(2,128)(2,1)S(1)}, u32[]{:S(2)}, u32[]{:S(2)}) %all-to-all-start.1) | async-done | bytes 49184 | tf_op jit(solution)/shard_map/all_to_all | solution.py:185
  239.3 5.0 all-to-all-start
  247.4 5.6 all-to-all-done
  253.0 209.6 %while.14 = (s32[]{:T(128)}, bf16[4,16,128]{2,1,0:T(8,128)(2,1)}, bf16[4,16,2,128,128]{4,3,2,1,0:T(8,128)(2,1)}, s32[4,16,10]{2,1,0:T(8,128)S(1)}, bf16[4,16,384...) while((s32[]{:T(128)}, bf16[4,16,128]{2,1,0:T(8,128)(2,1)}, ...), condition=%wide.region_13.14_spmd, body=%wide.region_10.13_spmd.sunk | while | flops 9330754 | bytes 80879120 | solution.py:192
  254.0 6.4 gather_fusion
  260.4 6.1 fusion.93
  266.5 6.7 copy.139
  273.3 7.3 squeeze.36
  284.3 6.7 copy.137
  291.0 7.3 squeeze.35
  298.3 3.4 fusion.100
  306.5 6.4 gather_fusion
  312.9 6.1 fusion.93
  319.0 6.7 copy.139
  325.7 7.3 squeeze.36
  336.7 6.7 copy.137
  343.5 7.3 squeeze.35
  350.8 3.4 fusion.100
  358.9 6.3 gather_fusion
  365.3 6.1 fusion.93
  371.4 6.7 copy.139
  378.1 7.3 squeeze.36
  389.1 6.7 copy.137
  395.8 7.3 squeeze.35
  403.1 3.4 fusion.100
  411.3 6.3 gather_fusion
  417.6 6.1 fusion.93
  423.7 6.7 copy.139
  430.4 7.3 squeeze.36
  441.4 6.7 copy.137
  448.1 7.3 squeeze.35
  455.4 3.4 fusion.100
  462.5 5.1 all-to-all-start.2
  470.4 6.9 all-to-all-done.2
  480.2 6.8 all-to-all-start.3
  488.4 58.4 %all-reduce.2.cloned.1.call-done = bf16[528,1024]{1,0:T(8,128)(2,1)} async-done(((bf16[528,1024]{1,0:T(8,128)(2,1)}), bf16[528,1024]{1,0:T(8,128)(2,1)}) %all-reduce.2.cloned.1.call-update) | async-done | bytes 1081360 | tf_op jit(solution)/shard_map/psum | solution.py:211
  548.5 19.2 %all-gather.7.cloned.1.call-done = bf16[1024,512]{1,0:T(8,128)(2,1)} async-done(((bf16[32,512]{1,0:T(8,128)(2,1)}), bf16[1024,512]{1,0:T(8,128)(2,1)}) %all-gather.7.cloned.1.call-update) | async-done | bytes 1048592 | tf_op jit(solution)/shard_map/all_gather | solution.py:217
  567.7 3.3 fusion.51
  571.0 73.5 %all-gather.11.cloned.1.call-done = bf16[512,1024]{0,1:T(8,128)(2,1)} async-done(((bf16[512,32]{0,1:T(8,128)(2,1)}), bf16[512,1024]{0,1:T(8,128)(2,1)}) %all-gather.11.cloned.1.call-update) | async-done | bytes 1048592 | tf_op jit(solution)/shard_map/all_gather | solution.py:226
  644.5 76.8 %all-gather.9.cloned.1.call-done = bf16[1024,512]{1,0:T(8,128)(2,1)} async-done(((bf16[32,512]{1,0:T(8,128)(2,1)}), bf16[1024,512]{1,0:T(8,128)(2,1)}) %all-gather.9.cloned.1.call-update) | async-done | bytes 1048592 | tf_op jit(solution)/shard_map/all_gather | solution.py:218
  721.3 4.6 convolution_convert_fusion.1
  729.3 32.6 %reduce-scatter.4.cloned.1.call-done = bf16[128,528]{1,0:T(8,128)(2,1)} async-done(((bf16[1024,528]{1,0:T(8,128)(2,1)}), bf16[128,528]{1,0:T(8,128)(2,1)}) %reduce-scatter.4.cloned.1.call-update) | async-done | bytes 135184
  763.7 3.8 gather_fusion.5
  (225 shorter events, 67.6 us)
Async XLA Ops:
  8.0 210.7 %copy-start.7 = (f32[1024]{0:T(1024)S(1)}, f32[1024]{0:T(1024)}, u32[]{:S(2)}) copy-start(f32[1024]{0:T(1024)} %param.32) | copy-start | bytes 12292
  8.0 209.0 %all-gather.5.cloned.1.call-start = ((), (), s32[]{:S(2)}) async-start(), calls=%async_computation.5 | async-start | bytes 1216512 | tf_op jit(solution)/shard_map/all_gather | solution.py:74
  217.0 3.5 copy-start.2
  221.4 22.9 %copy-start.5 = (f32[2]{0:T(128)S(1)}, f32[2]{0:T(128)}, u32[]{:S(2)}) copy-start(f32[2]{0:T(128)} %param.36) | copy-start | bytes 28
  221.4 22.9 %copy-start.6 = (f32[2]{0:T(128)S(1)}, f32[2]{0:T(128)}, u32[]{:S(2)}) copy-start(f32[2]{0:T(128)} %param.37) | copy-start | bytes 28
  223.5 15.8 %all-to-all-start.1 = ((bf16[32,2,384]{2,1,0:T(2,128)(2,1)}), bf16[32,2,384]{2,1,0:T(2,128)(2,1)S(1)}, u32[]{:S(2)}, u32[]{:S(2)}) async-start(bf16[32,2,384]{2,1,0:T(2,128)(2,1)} %reshape.400), calls=%async_computation.1 | async-start | bytes 98304 | tf_op jit(solution)/shard_map/all_to_all | solution.py:185
  239.3 13.7 %all-to-all-start = ((s32[32,2,10]{2,1,0:T(2,128)}), s32[32,2,10]{2,1,0:T(2,128)S(1)}, u32[]{:S(2)}, u32[]{:S(2)}) async-start(s32[32,2,10]{2,1,0:T(2,128)} %bitcast.30), calls=%async_computation | async-start | bytes 65536 | tf_op jit(solution)/shard_map/all_to_all | solution.py:186
  244.3 8.7 %copy-start = (bf16[32,2,128,128]{3,2,1,0:T(8,128)(2,1)S(1)}, bf16[32,2,128,128]{3,2,1,0:T(8,128)(2,1)}, u32[]{:S(2)}) copy-start(bf16[32,2,128,128]{3,2,1,0:T(8,128)(2,1)} %param.44) | copy-start | bytes 6291460
  244.3 8.7 %copy-start.1 = (s32[32,128]{1,0:T(8,128)S(1)}, s32[32,128]{1,0:T(8,128)}, u32[]{:S(2)}) copy-start(s32[32,128]{1,0:T(8,128)} %param.45) | copy-start | bytes 49156
  462.5 14.8 %all-to-all-start.2 = ((bf16[32,2,128]{2,1,0:T(2,128)(2,1)}), bf16[32,2,128]{2,1,0:T(2,128)(2,1)S(1)}, u32[]{:S(2)}, u32[]{:S(2)}) async-start(bf16[32,2,128]{2,1,0:T(2,128)(2,1)} %bitcast.34), calls=%async_computation.2 | async-start | bytes 32768 | tf_op jit(solution)/shard_map/all_to_all | solution.py:195
  467.6 79.2 %all-reduce.2.cloned.1.call-start = ((), (), s32[]{:S(2)}) async-start(), calls=%async_computation.6 | async-start | bytes 2162688 | tf_op jit(solution)/shard_map/psum | solution.py:211
  467.7 10.4 %copy-start.4 = (bf16[128,1024]{0,1:T(8,128)(2,1)S(1)}, bf16[128,1024]{0,1:T(8,128)(2,1)}, u32[]{:S(2)}) copy-start(bf16[128,1024]{0,1:T(8,128)(2,1)} %all_gather.28) | copy-start | bytes 786436
  479.6 88.1 %all-gather.7.cloned.1.call-start = ((), (), s32[]{:S(2)}) async-start(), calls=%async_computation.7 | async-start | bytes 1081344 | tf_op jit(solution)/shard_map/all_gather | solution.py:217
  480.2 66.7 %copy-start.3 = (bf16[528,1024]{1,0:T(8,128)(2,1)S(1)}, bf16[528,1024]{1,0:T(8,128)(2,1)}, u32[]{:S(2)}) copy-start(bf16[528,1024]{1,0:T(8,128)(2,1)} %all-gather.5.cloned.1.call-done) | copy-start | bytes 3244036
  480.2 283.5 %all-to-all-start.3 = ((bf16[32,2,2,128,128]{4,3,2,1,0:T(8,128)(2,1)}), bf16[32,2,2,128,128]{4,3,2,1,0:T(8,128)(2,1)}, u32[]{:S(2)}, u32[]{:S(2)}) async-start(bf16[32,2,2,128,128]{4,3,2,1,0:T(8,128)(2,1)} %bitcast.142), calls=%async_computation.3 | async-start | bytes 8388608 | tf_op jit(solution)/shard_map/all_to_all | solution.py:198
  487.0 157.5 %all-gather.11.cloned.1.call-start = ((), (), s32[]{:S(2)}) async-start(), calls=%async_computation.9 | async-start | bytes 1081344 | tf_op jit(solution)/shard_map/all_gather | solution.py:226
  487.6 233.7 %all-gather.9.cloned.1.call-start = ((), (), s32[]{:S(2)}) async-start(), calls=%async_computation.8 | async-start | bytes 1081344 | tf_op jit(solution)/shard_map/all_gather | solution.py:218
  488.1 79.6 %copy-start.8 = (f32[1024]{0:T(1024)S(1)}, f32[1024]{0:T(1024)}, u32[]{:S(2)}) copy-start(f32[1024]{0:T(1024)} %param.33) | copy-start | bytes 12292
  488.1 273.8 %reduce-scatter.4.cloned.1.call-start = ((), (), s32[]{:S(2)}) async-start(), calls=%async_computation.10 | async-start | bytes 1474560
Sparse Core Ops, SparseCore 0:
  10.7 28.8 all-gather.4
  479.7 67.0 all-reduce.1
  728.5 33.3 reduce-scatter.3
Sparse Core Ops, SparseCore 1:
  483.0 84.7 all-gather.6
  570.5 73.9 all-gather.10
  647.3 74.0 all-gather.8
where the time goes:
time: 778 us; the launch traced here: 775 us
  waiting for transfers between devices  284 us (37%)
  blocking collectives  198 us (25%)
  local copies, waits for them, and re-layouts  189 us (24%)
  matrix products  42.3 us (5%)
  starting transfers between devices  24.4 us (3%)
  other arithmetic  21.1 us (3%)
  between operations  15.7 us (2%)
    all_gather x1, waiting for transfers between devices, on_device(): lax.all_gather(w_up, 'col', axis=0, tiled=True)  76.8 us
    all_gather x1, waiting for transfers between devices, on_device(): lax.all_gather(w_down, 'col', axis=1, tiled=True)  73.5 us
    psum x1, waiting for transfers between devices, on_device(): lax.psum(partial_out.astype(jnp.bfloat16), 'row').astype(jnp.float32)  58.4 us
    while x8, local copies, waits for them, and re-layouts  53.9 us
    all_gather x1, blocking collectives, on_device(): lax.all_gather(w_k, 'col', axis=0, tiled=True)  51.9 us
    all_gather x1, blocking collectives, on_device(): lax.all_gather(w_o, 'col', axis=1, tiled=True)  51.4 us
    all_gather x1, blocking collectives, on_device(): lax.all_gather(w_v, 'col', axis=0, tiled=True)  47.7 us
    all_gather x1, blocking collectives, on_device(): lax.all_gather(w_q, 'col', axis=0, tiled=True)  47.2 us
  transfers between devices with their start and end apart: 10, of which 8 were waited for; matrix products, arithmetic and copies ran while one was open for 4% of the time, Pallas kernels for 0%

commit v1 on v0

--- a/solution.py
+++ b/solution.py
@@ -5,6 +5,13 @@
 
 HD = 64
 eps = 1e-05
+
+
+def gather_over(x, name, along):
+    size = lax.axis_size(name)
+    blocks = jnp.stack([x for _ in range(size)])
+    blocks = lax.all_to_all(blocks, name, split_axis=0, concat_axis=0)
+    return jnp.concatenate(blocks, axis=along)
 
 
 def as_sent(array):
@@ -74,7 +81,7 @@
     gathered_input = lax.all_gather(layer_input, "row", axis=1, tiled=True)
     normed = norm_rows(gathered_input.astype(jnp.float32), norm1).astype(jnp.bfloat16)
     pieces = (
-        lax.all_gather(w_q, "col", axis=0, tiled=True),
+        gather_over(w_q, "col", 0),
         lax.all_gather(w_k, "col", axis=0, tiled=True),
         lax.all_gather(w_v, "col", axis=0, tiled=True),
     )

time: 778 us -> 744 us (0.956)
  blocking collectives: 198 us -> 148 us
  starting transfers between devices: 24.4 us -> 37.9 us
    all_gather x1 -> x0, blocking collectives: 47.2 us -> none  [on_device(): lax.all_gather(w_q, 'col', axis=0, tiled=True)]
    all_to_all x0 -> x1, starting transfers between devices: none -> 11.7 us  [gather_over(): blocks = lax.all_to_all(blocks, name, split_axis=0, concat_axis=0)]
  transfers between devices with their start and end apart: 10 -> 11, of which waited for: 8 -> 8; matrix products, arithmetic and copies ran while one was open for 4% -> 4% of each run, Pallas kernels for 0% -> 0%
where the time goes in v1:
time: 744 us; the launch traced here: 741 us
  waiting for transfers between devices  285 us (38%)
  local copies, waits for them, and re-layouts  190 us (26%)
  blocking collectives  148 us (20%)
  matrix products  42.3 us (6%)
  starting transfers between devices  37.9 us (5%)
  other arithmetic  21.2 us (3%)
  between operations  15.8 us (2%)
    all_gather x1, waiting for transfers between devices, on_device(): lax.all_gather(w_up, 'col', axis=0, tiled=True)  76.8 us
    all_gather x1, waiting for transfers between devices, on_device(): lax.all_gather(w_down, 'col', axis=1, tiled=True)  73.5 us
    psum x1, waiting for transfers between devices, on_device(): lax.psum(partial_out.astype(jnp.bfloat16), 'row').astype(jnp.float32)  59.3 us
    while x8, local copies, waits for them, and re-layouts  53.9 us
    all_gather x1, blocking collectives, on_device(): lax.all_gather(w_o, 'col', axis=1, tiled=True)  51.7 us
    all_gather x1, blocking collectives, on_device(): lax.all_gather(w_k, 'col', axis=0, tiled=True)  48.6 us
    all_gather x1, blocking collectives, on_device(): lax.all_gather(w_v, 'col', axis=0, tiled=True)  47.3 us
    unnamed x7, waiting for transfers between devices  35 us
  transfers between devices with their start and end apart: 11, of which 8 were waited for; matrix products, arithmetic and copies ran while one was open for 4% of the time, Pallas kernels for 0%

profile of v1, /device:TPU:8, one launch (start us, length us, event | category | flops | bytes accessed | tf_op | source)
XLA Modules:
  0.0 740.9 jit_solution(14996291297350147445)
XLA Ops:
  10.2 11.7 %all-to-all-start = ((bf16[32,32,128]{2,1,0:T(8,128)(2,1)}), bf16[32,32,128]{2,1,0:T(8,128)(2,1)S(1)}, u32[]{:S(2)}, u32[]{:S(2)}) async-start(bf16[32,32,128]{2,1,0:T(8,128)(2,1)} %stack.19), calls=%async_computation | async-start | bytes 524288 | tf_op jit(solution)/shard_map/all_to_all | solution.py:13
  29.0 48.6 %all_gather.23 = bf16[1024,128]{1,0:T(8,128)(2,1)S(1)} all-gather(bf16[32,128]{1,0:T(8,128)(2,1)} %param.26), channel_id=1, replica_groups=mesh['row'=8,'col'=32] {'col'}, dimensions={0}, use_global_device_ids=true | all-gather | bytes 270336 | tf_op jit(solution)/shard_map/all_gather | solution.py:85
  77.6 47.3 %all_gather.22 = bf16[1024,128]{1,0:T(8,128)(2,1)S(1)} all-gather(bf16[32,128]{1,0:T(8,128)(2,1)} %param.27), channel_id=1, replica_groups=mesh['row'=8,'col'=32] {'col'}, dimensions={0}, use_global_device_ids=true | all-gather | bytes 270336 | tf_op jit(solution)/shard_map/all_gather | solution.py:86
  126.4 51.7 %all_gather.24 = bf16[128,1024]{0,1:T(8,128)(2,1)} all-gather(bf16[128,32]{0,1:T(8,128)(2,1)} %param.28), channel_id=1, replica_groups=mesh['row'=8,'col'=32] {'col'}, dimensions={1}, use_global_device_ids=true | all-gather | bytes 270336 | tf_op jit(solution)/shard_map/all_gather | solution.py:214
  186.2 8.2 %all-to-all-start.2 = ((bf16[32,2,384]{2,1,0:T(2,128)(2,1)}), bf16[32,2,384]{2,1,0:T(2,128)(2,1)S(1)}, u32[]{:S(2)}, u32[]{:S(2)}) async-start(bf16[32,2,384]{2,1,0:T(2,128)(2,1)} %reshape.404), calls=%async_computation.2 | async-start | bytes 98304 | tf_op jit(solution)/shard_map/all_to_all | solution.py:192
  194.4 8.7 %all-to-all-done.2 = bf16[32,2,384]{2,1,0:T(2,128)(2,1)S(1)} async-done(((bf16[32,2,384]{2,1,0:T(2,128)(2,1)}), bf16[32,2,384]{2,1,0:T(2,128)(2,1)S(1)}, u32[]{:S(2)}, u32[]{:S(2)}) %all-to-all-start.2) | async-done | bytes 49184 | tf_op jit(solution)/shard_map/all_to_all | solution.py:192
  203.1 5.0 all-to-all-start.1
  211.2 5.6 all-to-all-done.1
  216.8 209.6 %while.14 = (s32[]{:T(128)}, bf16[4,16,128]{2,1,0:T(8,128)(2,1)}, bf16[4,16,2,128,128]{4,3,2,1,0:T(8,128)(2,1)}, s32[4,16,10]{2,1,0:T(8,128)S(1)}, bf16[4,16,384...) while((s32[]{:T(128)}, bf16[4,16,128]{2,1,0:T(8,128)(2,1)}, ...), condition=%wide.region_13.14_spmd, body=%wide.region_10.13_spmd.sunk | while | flops 9330754 | bytes 80879120 | solution.py:199
  217.9 6.4 gather_fusion
  224.3 6.1 fusion.94
  230.4 6.7 copy.138
  237.1 7.3 squeeze.36
  248.1 6.7 copy.136
  254.8 7.3 squeeze.35
  262.2 3.4 fusion.101
  270.4 6.4 gather_fusion
  276.7 6.1 fusion.94
  282.8 6.7 copy.138
  289.6 7.3 squeeze.36
  300.6 6.7 copy.136
  307.3 7.3 squeeze.35
  314.6 3.4 fusion.101
  322.8 6.3 gather_fusion
  329.1 6.1 fusion.94
  335.2 6.7 copy.138
  341.9 7.3 squeeze.36
  352.9 6.7 copy.136
  359.7 7.3 squeeze.35
  367.0 3.4 fusion.101
  375.2 6.3 gather_fusion
  381.4 6.1 fusion.94
  387.5 6.7 copy.138
  394.3 7.3 squeeze.36
  405.3 6.7 copy.136
  412.0 7.3 squeeze.35
  419.3 3.4 fusion.101
  426.4 5.1 all-to-all-start.3
  434.3 6.5 all-to-all-done.3
  443.6 7.5 %all-to-all-start.4 = ((bf16[32,2,2,128,128]{4,3,2,1,0:T(8,128)(2,1)}), bf16[32,2,2,128,128]{4,3,2,1,0:T(8,128)(2,1)}, u32[]{:S(2)}, u32[]{:S(2)}) async-start(bf16[32,2,2,128,128]{4,3,2,1,0:T(8,128)(2,1)} %bitcast.148), calls=%async_computation.4 | async-start | bytes 8388608 | tf_op jit(solution)/shard_map/all_to_all | solution.py:205
  452.5 59.3 %all-reduce.2.cloned.1.call-done = bf16[528,1024]{1,0:T(8,128)(2,1)} async-done(((bf16[528,1024]{1,0:T(8,128)(2,1)}), bf16[528,1024]{1,0:T(8,128)(2,1)}) %all-reduce.2.cloned.1.call-update) | async-done | bytes 1081360 | tf_op jit(solution)/shard_map/psum | solution.py:218
  513.6 20.2 %all-gather.7.cloned.1.call-done = bf16[1024,512]{1,0:T(8,128)(2,1)} async-done(((bf16[32,512]{1,0:T(8,128)(2,1)}), bf16[1024,512]{1,0:T(8,128)(2,1)}) %all-gather.7.cloned.1.call-update) | async-done | bytes 1048592 | tf_op jit(solution)/shard_map/all_gather | solution.py:224
  533.8 3.3 fusion.53
  537.1 73.5 %all-gather.11.cloned.1.call-done = bf16[512,1024]{0,1:T(8,128)(2,1)} async-done(((bf16[512,32]{0,1:T(8,128)(2,1)}), bf16[512,1024]{0,1:T(8,128)(2,1)}) %all-gather.11.cloned.1.call-update) | async-done | bytes 1048592 | tf_op jit(solution)/shard_map/all_gather | solution.py:233
  610.6 76.8 %all-gather.9.cloned.1.call-done = bf16[1024,512]{1,0:T(8,128)(2,1)} async-done(((bf16[32,512]{1,0:T(8,128)(2,1)}), bf16[1024,512]{1,0:T(8,128)(2,1)}) %all-gather.9.cloned.1.call-update) | async-done | bytes 1048592 | tf_op jit(solution)/shard_map/all_gather | solution.py:225
  687.4 4.6 convolution_convert_fusion.1
  695.3 32.7 %reduce-scatter.4.cloned.1.call-done = bf16[128,528]{1,0:T(8,128)(2,1)} async-done(((bf16[1024,528]{1,0:T(8,128)(2,1)}), bf16[128,528]{1,0:T(8,128)(2,1)}) %reduce-scatter.4.cloned.1.call-update) | async-done | bytes 135184
  729.8 3.8 gather_fusion.5
  (228 shorter events, 69.2 us)
Async XLA Ops:
  8.0 173.4 %copy-start.7 = (f32[1024]{0:T(1024)S(1)}, f32[1024]{0:T(1024)}, u32[]{:S(2)}) copy-start(f32[1024]{0:T(1024)} %param.32) | copy-start | bytes 12292
  8.0 171.7 %all-gather.5.cloned.1.call-start = ((), (), s32[]{:S(2)}) async-start(), calls=%async_computation.6 | async-start | bytes 1216512 | tf_op jit(solution)/shard_map/all_gather | solution.py:81
  10.2 169.4 %all-to-all-start = ((bf16[32,32,128]{2,1,0:T(8,128)(2,1)}), bf16[32,32,128]{2,1,0:T(8,128)(2,1)S(1)}, u32[]{:S(2)}, u32[]{:S(2)}) async-start(bf16[32,32,128]{2,1,0:T(8,128)(2,1)} %stack.19), calls=%async_computation | async-start | bytes 524288 | tf_op jit(solution)/shard_map/all_to_all | solution.py:13
  179.7 3.5 copy-start.2
  184.1 24.0 %copy-start.5 = (f32[2]{0:T(128)S(1)}, f32[2]{0:T(128)}, u32[]{:S(2)}) copy-start(f32[2]{0:T(128)} %param.36) | copy-start | bytes 28
  184.1 24.0 %copy-start.6 = (f32[2]{0:T(128)S(1)}, f32[2]{0:T(128)}, u32[]{:S(2)}) copy-start(f32[2]{0:T(128)} %param.37) | copy-start | bytes 28
  186.2 16.9 %all-to-all-start.2 = ((bf16[32,2,384]{2,1,0:T(2,128)(2,1)}), bf16[32,2,384]{2,1,0:T(2,128)(2,1)S(1)}, u32[]{:S(2)}, u32[]{:S(2)}) async-start(bf16[32,2,384]{2,1,0:T(2,128)(2,1)} %reshape.404), calls=%async_computation.2 | async-start | bytes 98304 | tf_op jit(solution)/shard_map/all_to_all | solution.py:192
  203.1 13.7 %all-to-all-start.1 = ((s32[32,2,10]{2,1,0:T(2,128)}), s32[32,2,10]{2,1,0:T(2,128)S(1)}, u32[]{:S(2)}, u32[]{:S(2)}) async-start(s32[32,2,10]{2,1,0:T(2,128)} %bitcast.33), calls=%async_computation.1 | async-start | bytes 65536 | tf_op jit(solution)/shard_map/all_to_all | solution.py:193
  208.1 8.7 %copy-start = (bf16[32,2,128,128]{3,2,1,0:T(8,128)(2,1)S(1)}, bf16[32,2,128,128]{3,2,1,0:T(8,128)(2,1)}, u32[]{:S(2)}) copy-start(bf16[32,2,128,128]{3,2,1,0:T(8,128)(2,1)} %param.44) | copy-start | bytes 6291460
  208.1 8.7 %copy-start.1 = (s32[32,128]{1,0:T(8,128)S(1)}, s32[32,128]{1,0:T(8,128)}, u32[]{:S(2)}) copy-start(s32[32,128]{1,0:T(8,128)} %param.45) | copy-start | bytes 49156
  426.4 14.4 %all-to-all-start.3 = ((bf16[32,2,128]{2,1,0:T(2,128)(2,1)}), bf16[32,2,128]{2,1,0:T(2,128)(2,1)S(1)}, u32[]{:S(2)}, u32[]{:S(2)}) async-start(bf16[32,2,128]{2,1,0:T(2,128)(2,1)} %bitcast.37), calls=%async_computation.3 | async-start | bytes 32768 | tf_op jit(solution)/shard_map/all_to_all | solution.py:202
  431.5 80.4 %all-reduce.2.cloned.1.call-start = ((), (), s32[]{:S(2)}) async-start(), calls=%async_computation.7 | async-start | bytes 2162688 | tf_op jit(solution)/shard_map/psum | solution.py:218
  431.5 9.9 %copy-start.4 = (bf16[128,1024]{0,1:T(8,128)(2,1)S(1)}, bf16[128,1024]{0,1:T(8,128)(2,1)}, u32[]{:S(2)}) copy-start(bf16[128,1024]{0,1:T(8,128)(2,1)} %all_gather.24) | copy-start | bytes 786436
  443.0 90.8 %all-gather.7.cloned.1.call-start = ((), (), s32[]{:S(2)}) async-start(), calls=%async_computation.8 | async-start | bytes 1081344 | tf_op jit(solution)/shard_map/all_gather | solution.py:224
  443.6 68.3 %copy-start.3 = (bf16[528,1024]{1,0:T(8,128)(2,1)S(1)}, bf16[528,1024]{1,0:T(8,128)(2,1)}, u32[]{:S(2)}) copy-start(bf16[528,1024]{1,0:T(8,128)(2,1)} %all-gather.5.cloned.1.call-done) | copy-start | bytes 3244036
  443.6 286.2 %all-to-all-start.4 = ((bf16[32,2,2,128,128]{4,3,2,1,0:T(8,128)(2,1)}), bf16[32,2,2,128,128]{4,3,2,1,0:T(8,128)(2,1)}, u32[]{:S(2)}, u32[]{:S(2)}) async-start(bf16[32,2,2,128,128]{4,3,2,1,0:T(8,128)(2,1)} %bitcast.148), calls=%async_computation.4 | async-start | bytes 8388608 | tf_op jit(solution)/shard_map/all_to_all | solution.py:205
  451.1 159.5 %all-gather.11.cloned.1.call-start = ((), (), s32[]{:S(2)}) async-start(), calls=%async_computation.10 | async-start | bytes 1081344 | tf_op jit(solution)/shard_map/all_gather | solution.py:233
  451.7 235.7 %all-gather.9.cloned.1.call-start = ((), (), s32[]{:S(2)}) async-start(), calls=%async_computation.9 | async-start | bytes 1081344 | tf_op jit(solution)/shard_map/all_gather | solution.py:225
  452.3 81.5 %copy-start.8 = (f32[1024]{0:T(1024)S(1)}, f32[1024]{0:T(1024)}, u32[]{:S(2)}) copy-start(f32[1024]{0:T(1024)} %param.33) | copy-start | bytes 12292
  452.3 275.7 %reduce-scatter.4.cloned.1.call-start = ((), (), s32[]{:S(2)}) async-start(), calls=%async_computation.11 | async-start | bytes 1474560
Sparse Core Ops, SparseCore 0:
  10.7 28.8 all-gather.4
  443.1 68.6 all-reduce.1
  694.5 33.4 reduce-scatter.3
Sparse Core Ops, SparseCore 1:
  446.4 87.3 all-gather.6
  536.6 73.9 all-gather.10
  613.3 74.0 all-gather.8
